TPU v7x, 32 devices: a whole 2x2x4 slice. The times are simulated.
32 devices in a mesh: tile: 8 (over z, y), src: 4 (over x, core).
Axes of the slice: x: 2, y: 2, z: 4, core: 2. Of those that a mesh axis runs over, the one named last changes fastest.
Arguments:
- excitation: bfloat16 [2, 512, 8192], P(None, 'src', 'tile'), may hold values from -6 to 6
- near_blocks: bfloat16 [16, 3, 2, 512, 512], P('tile'), may hold values from -0.02734375 to 0.02734375
- source_basis: bfloat16 [16, 2, 24, 512], P('tile'), may hold values from -0.1875 to 0.1875
- target_basis: bfloat16 [16, 2, 24, 512], P('tile'), may hold values from -0.625 to 0.625
- coupling: bfloat16 [2, 384, 384], P(None, None, 'tile'), may hold values from -0.109375 to 0.109375
- pair_rank: int32 [16, 16], P(None, 'tile'), may hold values from 2 to 24
- far_link: int32 [16, 16], P(None, 'tile'), may hold values 0 or 1
- focal_kernel: bfloat16 [2, 64, 8192], P(None, None, 'tile'), may hold values from -0.046875 to 0.046875
- focal_target: float32 [64], replicated, may hold values from 0.3 to 0.9
- focal_owner: int32 [64], replicated, may hold values from 0 to 63, each once
Outputs:
- field: float32 [2, 512, 8192], P(None, 'src', 'tile')
- focal_residual: float32 [64], P('tile')
- adjoint: float32 [2, 512, 8192], P(None, 'src', 'tile')
Inputs may be any that keep to these rules, and one draw needn't show every extreme that they name: `focal_owner`: each focal point has its own slot; slot k belongs to index k // 8 of tile.
All inputs are finite; a program needn't handle non-finite values. No bound on the sum of `far_link` on one device may be relied on, other than what follows from the above.
Results may differ from a plain program's by a relative error of at most 0.006.
Values may be sent and summed in bfloat16 or wider, within the bound.
No kernel may reach another device: no remote copies, remote signals or barrier semaphores. Data moves between devices by JAX's collectives and lax.ppermute only.
A program may use at most 64 MiB of HBM per device.

v0:
```python
import jax
import jax.numpy as jnp
from jax import lax
from jax.sharding import PartitionSpec as P

TILE = 512
RANK = 24
DAMPING = 0.8


def extended(x, sides, width):
    for axis, dim in sides:
        size, length = (lax.axis_size(axis), x.shape[dim])
        up = [(i, (i + 1) % size) for i in range(size)]
        down = [(j, i) for i, j in up]
        last = lax.slice_in_dim(x, length - width, length, axis=dim)
        initial = lax.slice_in_dim(x, 0, width, axis=dim)
        before = lax.ppermute(last, axis, up)
        after = lax.ppermute(initial, axis, down)
        x = jnp.concatenate([before, x, after], axis=dim)
    return x


def plain_dot(left, right, contract):
    return lax.dot_general(
        left, right, (((1,), (contract,)), ((), ())), preferred_element_type=jnp.float32
    )


def complex_dot(left_re, left_im, right_re, right_im, contract):
    real_part = plain_dot(left_re, right_re, contract) - plain_dot(left_im, right_im, contract)
    imag_part = plain_dot(left_re, right_im, contract) + plain_dot(left_im, right_re, contract)
    return (real_part, imag_part)


def per_device(
    excitation,
    near_blocks,
    source_basis,
    target_basis,
    coupling,
    pair_rank,
    far_link,
    focal_kernel,
    focal_target,
    focal_owner,
):
    tile_count = near_blocks.shape[0]
    src_rows = excitation.shape[1]
    tiles = pair_rank.shape[0]
    focal_count = focal_target.shape[0]
    first_tile = lax.axis_index("tile") * tile_count
    global_tiles = first_tile + jnp.arange(tile_count)
    source_tiles = jnp.arange(tiles)[:, None]
    distance = (global_tiles[None, :] - source_tiles) % tiles
    far_pairs = (far_link == 1) & (distance != 0) & (distance != 1) & (distance != tiles - 1)
    levels = jnp.arange(RANK)
    rank_limit = pair_rank[:, None, :, None]
    rank_mask = (
        far_pairs[:, None, :, None]
        & (levels[None, :, None, None] < rank_limit)
        & (levels[None, None, None, :] < rank_limit)
    )
    rank_mask = rank_mask.reshape(tiles * RANK, tile_count * RANK)
    masked = coupling * rank_mask.astype(coupling.dtype)
    flipped = lax.all_to_all(masked, "tile", split_axis=1, concat_axis=2, tiled=True)

    def apply_transpose(field):
        field_bf = field.astype(jnp.bfloat16)
        moved_re = [[], [], []]
        moved_im = [[], [], []]
        proj_re = []
        proj_im = []
        for tile_here in range(tile_count):
            own = field_bf[:, :, tile_here * TILE : (tile_here + 1) * TILE]
            for offset in range(3):
                part_re, part_im = complex_dot(
                    own[0],
                    own[1],
                    near_blocks[tile_here, offset, 0],
                    near_blocks[tile_here, offset, 1],
                    1,
                )
                moved_re[offset].append(part_re)
                moved_im[offset].append(part_im)
            part_re, part_im = complex_dot(
                own[0], own[1], target_basis[tile_here, 0], target_basis[tile_here, 1], 1
            )
            proj_re.append(part_re)
            proj_im.append(part_im)
        moved = [
            jnp.stack([jnp.concatenate(moved_re[k], axis=1), jnp.concatenate(moved_im[k], axis=1)])
            for k in range(3)
        ]
        width = tile_count * TILE
        edges = jnp.concatenate([moved[0][:, :, 0:TILE], moved[2][:, :, width - TILE :]], axis=2)
        arrived = extended(edges.astype(jnp.bfloat16), (("tile", 2),), TILE).astype(edges.dtype)
        from_left = jnp.concatenate(
            [arrived[:, :, 0:TILE], moved[2][:, :, 0 : width - TILE]], axis=2
        )
        from_right = jnp.concatenate(
            [moved[0][:, :, TILE:], arrived[:, :, 3 * TILE : 4 * TILE]], axis=2
        )
        near_part = moved[1] + from_left + from_right
        projected = jnp.stack(
            [jnp.concatenate(proj_re, axis=1), jnp.concatenate(proj_im, axis=1)]
        ).astype(jnp.bfloat16)
        shard_piece = lax.all_gather(projected, "tile", axis=2, tiled=True)
        term_re, term_im = complex_dot(shard_piece[0], shard_piece[1], flipped[0], flipped[1], 1)
        summed_back = jnp.stack([term_re, term_im]).astype(jnp.bfloat16)
        far_re = []
        far_im = []
        for tile_here in range(tile_count):
            piece = summed_back[:, :, tile_here * RANK : (tile_here + 1) * RANK]
            part_re, part_im = complex_dot(
                piece[0], piece[1], source_basis[tile_here, 0], source_basis[tile_here, 1], 0
            )
            far_re.append(part_re)
            far_im.append(part_im)
        far_part = jnp.stack([jnp.concatenate(far_re, axis=1), jnp.concatenate(far_im, axis=1)])
        return field + near_part + far_part

    right_side = excitation.astype(jnp.float32)
    field = right_side
    for update in range(2):
        apply_field_bf = field.astype(jnp.bfloat16)
        padded = extended(apply_field_bf, (("tile", 2),), TILE)
        coeff_re = []
        coeff_im = []
        for apply_tile_here in range(tile_count):
            apply_own = apply_field_bf[:, :, apply_tile_here * TILE : (apply_tile_here + 1) * TILE]
            apply_part_re, apply_part_im = complex_dot(
                apply_own[0],
                apply_own[1],
                source_basis[apply_tile_here, 0],
                source_basis[apply_tile_here, 1],
                1,
            )
            coeff_re.append(apply_part_re)
            coeff_im.append(apply_part_im)
        coeff = jnp.stack(
            [jnp.concatenate(coeff_re, axis=1), jnp.concatenate(coeff_im, axis=1)]
        ).astype(jnp.bfloat16)
        fold_shard_piece = lax.all_gather(coeff, "tile", axis=2, tiled=True)
        fold_term_re, fold_term_im = complex_dot(
            fold_shard_piece[0], fold_shard_piece[1], masked[0], masked[1], 0
        )
        coupled = jnp.stack([fold_term_re, fold_term_im]).astype(jnp.bfloat16)
        out_re = []
        out_im = []
        for apply_tile_here in range(tile_count):
            total_re = jnp.zeros((src_rows, TILE), jnp.float32)
            total_im = jnp.zeros((src_rows, TILE), jnp.float32)
            for apply_offset in range(3):
                window = padded[
                    :,
                    :,
                    (apply_tile_here + apply_offset)
                    * TILE : (apply_tile_here + apply_offset + 1)
                    * TILE,
                ]
                apply_part_re, apply_part_im = complex_dot(
                    window[0],
                    window[1],
                    near_blocks[apply_tile_here, apply_offset, 0],
                    near_blocks[apply_tile_here, apply_offset, 1],
                    0,
                )
                total_re = total_re + apply_part_re
                total_im = total_im + apply_part_im
            apply_piece = coupled[:, :, apply_tile_here * RANK : (apply_tile_here + 1) * RANK]
            apply_part_re, apply_part_im = complex_dot(
                apply_piece[0],
                apply_piece[1],
                target_basis[apply_tile_here, 0],
                target_basis[apply_tile_here, 1],
                0,
            )
            out_re.append(total_re + apply_part_re)
            out_im.append(total_im + apply_part_im)
        added = jnp.stack([jnp.concatenate(out_re, axis=1), jnp.concatenate(out_im, axis=1)])
        field = field + DAMPING * (right_side - (field + added))
    field_bf = field.astype(jnp.bfloat16)
    focal_re, focal_im = complex_dot(field_bf[0], field_bf[1], focal_kernel[0], focal_kernel[1], 1)
    slots_here = focal_count // lax.axis_size("tile")
    first_slot = lax.axis_index("tile") * slots_here
    sources = src_rows * lax.axis_size("src")
    permute = (focal_owner[:, None] == jnp.arange(focal_count)[None, :]).astype(jnp.float32)
    summed_focal = lax.psum(jnp.stack([focal_re, focal_im]), "tile")
    intensity = lax.psum(
        jnp.sum(summed_focal[0] * summed_focal[0] + summed_focal[1] * summed_focal[1], axis=0),
        "src",
    )
    residual_part = jnp.tanh(intensity / (2.0 * sources)) - focal_target
    weights_re = (residual_part * summed_focal[0]).astype(jnp.bfloat16)
    weights_im = (-residual_part * summed_focal[1]).astype(jnp.bfloat16)
    residual_slots = jnp.dot(residual_part, permute, precision=lax.Precision.HIGHEST)
    residual_out = lax.dynamic_slice_in_dim(residual_slots, first_slot, slots_here)
    scale_factor = (tiles * TILE / focal_count) ** 0.5
    term_re, term_im = complex_dot(weights_re, weights_im, focal_kernel[0], focal_kernel[1], 0)
    source_term = jnp.stack([term_re, term_im]) * scale_factor
    adjoint = source_term + DAMPING * (source_term - apply_transpose(source_term))
    return (field, residual_out, adjoint)


def solution(mesh):
    return jax.shard_map(
        per_device,
        mesh=mesh,
        in_specs=(
            P(None, "src", "tile"),
            P("tile", None, None, None, None),
            P("tile", None, None, None),
            P("tile", None, None, None),
            P(None, None, "tile"),
            P(None, "tile"),
            P(None, "tile"),
            P(None, None, "tile"),
            P(),
            P(),
        ),
        out_specs=(P(None, "src", "tile"), P("tile"), P(None, "src", "tile")),
        check_vma=False,
    )
```

profile of v0, /device:TPU:0, one launch (start us, length us, event | category | flops | bytes accessed | tf_op | source)
XLA Modules:
  0.0 293.0 jit_solution(17563514672564382302)
XLA Ops:
  7.2 2.0 fusion.459
  9.1 6.0 %collective-permute-start.1 = (bf16[2,128,512]{2,1,0:T(8,128)(2,1)}, bf16[2,128,512]{2,1,0:T(8,128)(2,1)}, u32[]{:S(2)}, u32[]{:S(2)}) collective-permute-start(bf16[2,128,512]{2,1,0:T(8,128)(2,1)} %get-tuple-element.12), channel_id=1, source_target_pairs={{4,0},{8,4},{12,8},{16,12},{20,16},{24,20},{28,24},{0,28},{5,1},{9... | collective-permute-start | bytes 786440 | tf_op jit(solution)/shard_map/ppermute | solution.py:19
  19.8 6.0 %all-to-all-start = ((bf16[8,2,2304]{2,1,0:T(2,128)(2,1)}), bf16[8,2,2304]{2,1,0:T(2,128)(2,1)S(1)}, u32[]{:S(2)}, u32[]{:S(2)}) async-start(bf16[8,2,2304]{2,1,0:T(2,128)(2,1)} %reshape.84), calls=%async_computation | async-start | bytes 147456 | tf_op jit(solution)/shard_map/all_to_all | solution.py:66
  34.8 31.3 %all_gather.9 = bf16[2,128,384]{1,2,0:T(8,128)(2,1)S(1)} all-gather(bf16[2,128,48]{1,2,0:T(8,128)(2,1)S(1)} %pad_maximum_fusion.6), channel_id=1, replica_groups=mesh['tile'=8,'src'=4] {'tile'}, dimensions={2}, use_global_device_ids=true | all-gather | bytes 221184 | tf_op jit(solution)/shard_map/all_gather | solution.py:144
  66.3 1.3 fusion.94
  67.7 1.3 fusion.112
  84.3 1.8 fusion.85
  86.1 1.3 fusion.175
  87.4 1.5 fusion.20
  88.9 1.5 fusion.22
  90.5 1.3 fusion.77
  96.9 30.7 %all_gather.10 = bf16[2,128,384]{1,2,0:T(8,128)(2,1)S(1)} all-gather(bf16[2,128,48]{1,2,0:T(8,128)(2,1)S(1)} %pad_maximum_fusion.7), channel_id=1, replica_groups=mesh['tile'=8,'src'=4] {'tile'}, dimensions={2}, use_global_device_ids=true | all-gather | bytes 221184 | tf_op jit(solution)/shard_map/all_gather | solution.py:144
  131.0 4.0 %collective-permute-start.3 = (bf16[2,128,512]{2,1,0:T(8,128)(2,1)S(1)}, bf16[2,128,512]{2,1,0:T(8,128)(2,1)S(1)}, u32[]{:S(2)}, u32[]{:S(2)}) collective-permute-start(bf16[2,128,512]{2,1,0:T(8,128)(2,1)S(1)} %get-tuple-element.10), channel_id=1, source_target_pairs={{4,0},{8,4},{12,8},{16,12},{20,16},{24,20},{28,24},{0,28},{5,1},{9... | collective-permute-start | bytes 786440 | tf_op jit(solution)/shard_map/ppermute | solution.py:19
  139.2 5.9 %collective-permute-done.2 = bf16[2,128,512]{2,1,0:T(8,128)(2,1)S(1)} collective-permute-done((bf16[2,128,512]{2,1,0:T(8,128)(2,1)S(1)}, bf16[2,128,512]{2,1,0:T(8,128)(2,1)S(1)}, u32[]{:S(2)}, u32[]{:S(2)}) %collective-permute-start.2) | collective-permute-done | bytes 262176 | tf_op jit(solution)/shard_map/ppermute | solution.py:18
  150.1 66.4 %all-reduce.2.cloned.1.call-done = f32[2,128,64]{1,2,0:T(8,128)} async-done(((f32[2,128,64]{1,2,0:T(8,128)}), f32[2,128,64]{1,2,0:T(8,128)}) %all-reduce.2.cloned.1.call-update) | async-done | bytes 65552 | tf_op jit(solution)/shard_map/psum | solution.py:189
  217.4 5.8 %psum.15 = f32[64]{0:T(128)S(1)} all-reduce(f32[64]{0:T(128)S(1)} %add_reduce_fusion), channel_id=1, replica_groups=mesh['tile'=8,'src'=4] {'src'}, use_global_device_ids=true, to_apply=%region_2.3 | all-reduce | flops 64 | bytes 512 | tf_op jit(solution)/shard_map/psum | solution.py:190
  227.9 1.3 fusion.106
  229.2 1.4 fusion.160
  230.6 1.3 fusion.116
  236.1 30.7 %all_gather.11 = bf16[2,128,384]{1,2,0:T(8,128)(2,1)S(1)} all-gather(bf16[2,128,48]{1,2,0:T(8,128)(2,1)S(1)} %pad_maximum_fusion.8), channel_id=1, replica_groups=mesh['tile'=8,'src'=4] {'tile'}, dimensions={2}, use_global_device_ids=true | all-gather | bytes 221184 | tf_op jit(solution)/shard_map/all_gather | solution.py:108
  272.0 3.3 %collective-permute-start.5 = (bf16[2,128,512]{2,1,0:T(8,128)(2,1)S(1)}, bf16[2,128,512]{2,1,0:T(8,128)(2,1)S(1)}, u32[]{:S(2)}, u32[]{:S(2)}) collective-permute-start(bf16[2,128,512]{2,1,0:T(8,128)(2,1)S(1)} %fusion.67), channel_id=1, source_target_pairs={{4,0},{8,4},{12,8},{16,12},{20,16},{24,20},{28,24},{0,28},{5,1},{9... | collective-permute-start | bytes 786440 | tf_op jit(solution)/shard_map/ppermute | solution.py:19
  277.4 2.2 collective-permute-done.5
  279.7 4.8 %collective-permute-done.4 = bf16[2,128,512]{2,1,0:T(8,128)(2,1)S(1)} collective-permute-done((bf16[2,128,512]{2,1,0:T(8,128)(2,1)S(1)}, bf16[2,128,512]{2,1,0:T(8,128)(2,1)S(1)}, u32[]{:S(2)}, u32[]{:S(2)}) %collective-permute-start.4) | collective-permute-done | bytes 262176 | tf_op jit(solution)/shard_map/ppermute | solution.py:18
  284.6 1.6 fusion.61
  (219 shorter events, 62.8 us)
Async XLA Ops:
  7.2 62.5 %copy-start.1 = (bf16[2,128,1024]{2,1,0:T(8,128)(2,1)S(1)}, bf16[2,128,1024]{2,1,0:T(8,128)(2,1)}, u32[]{:S(2)}) copy-start(bf16[2,128,1024]{2,1,0:T(8,128)(2,1)} %param.10) | copy-start | bytes 1572868
  7.2 62.0 %copy-start.2 = (bf16[2,2,24,512]{3,2,1,0:T(8,128)(2,1)S(1)}, bf16[2,2,24,512]{3,2,1,0:T(8,128)(2,1)}, u32[]{:S(2)}) copy-start(bf16[2,2,24,512]{3,2,1,0:T(8,128)(2,1)} %param.13) | copy-start | bytes 294916
  9.1 75.1 %collective-permute-start.1 = (bf16[2,128,512]{2,1,0:T(8,128)(2,1)}, bf16[2,128,512]{2,1,0:T(8,128)(2,1)}, u32[]{:S(2)}, u32[]{:S(2)}) collective-permute-start(bf16[2,128,512]{2,1,0:T(8,128)(2,1)} %get-tuple-element.12), channel_id=1, source_target_pairs={{4,0},{8,4},{12,8},{16,12},{20,16},{24,20},{28,24},{0,28},{5,1},{9... | collective-permute-start | bytes 786440 | tf_op jit(solution)/shard_map/ppermute | solution.py:19
  15.2 70.9 %collective-permute-start = (bf16[2,128,512]{2,1,0:T(8,128)(2,1)}, bf16[2,128,512]{2,1,0:T(8,128)(2,1)}, u32[]{:S(2)}, u32[]{:S(2)}) collective-permute-start(bf16[2,128,512]{2,1,0:T(8,128)(2,1)} %get-tuple-element.11), channel_id=1, source_target_pairs={{0,4},{4,8},{8,12},{12,16},{16,20},{20,24},{24,28},{28,0},{1,5},{5... | collective-permute-start | bytes 786440 | tf_op jit(solution)/shard_map/ppermute | solution.py:18
  19.8 62.4 %all-to-all-start = ((bf16[8,2,2304]{2,1,0:T(2,128)(2,1)}), bf16[8,2,2304]{2,1,0:T(2,128)(2,1)S(1)}, u32[]{:S(2)}, u32[]{:S(2)}) async-start(bf16[8,2,2304]{2,1,0:T(2,128)(2,1)} %reshape.84), calls=%async_computation | async-start | bytes 147456 | tf_op jit(solution)/shard_map/all_to_all | solution.py:66
  25.8 190.7 %all-reduce.2.cloned.1.call-start = ((), (), s32[]{:S(2)}) async-start(), calls=%async_computation.1 | async-start | bytes 131072 | tf_op jit(solution)/shard_map/psum | solution.py:189
  25.8 46.6 %copy-start = (bf16[2,3,2,512,512]{4,3,2,1,0:T(8,128)(2,1)S(1)}, bf16[2,3,2,512,512]{4,3,2,1,0:T(8,128)(2,1)}, u32[]{:S(2)}) copy-start(bf16[2,3,2,512,512]{4,3,2,1,0:T(8,128)(2,1)} %param.11) | copy-start | bytes 18874372
  77.7 14.1 %slice-start = ((s8[6291456]{0:T(1024)(128)(4,1)}), s8[2097152]{0:T(1024)(128)(4,1)S(1)}, s32[]{:S(2)}) async-start(s8[6291456]{0:T(1024)(128)(4,1)} %bitcast.613), calls=%async_computation.2 | async-start | bytes 4194304
  83.1 9.9 %copy-start.6 = (f32[128,512]{1,0:T(8,128)S(1)}, f32[128,512]{1,0:T(8,128)}, u32[]{:S(2)}) copy-start(f32[128,512]{1,0:T(8,128)} %convolution_subtract_fusion.23) | copy-start | bytes 786436
  83.1 9.9 %copy-start.7 = (f32[128,512]{1,0:T(8,128)S(1)}, f32[128,512]{1,0:T(8,128)}, u32[]{:S(2)}) copy-start(f32[128,512]{1,0:T(8,128)} %fusion.3) | copy-start | bytes 786436
  83.1 11.1 %copy-start.4 = (f32[128,512]{1,0:T(8,128)S(1)}, f32[128,512]{1,0:T(8,128)}, u32[]{:S(2)}) copy-start(f32[128,512]{1,0:T(8,128)} %convolution_subtract_fusion.16) | copy-start | bytes 786436
  83.1 11.1 %copy-start.5 = (f32[128,512]{1,0:T(8,128)S(1)}, f32[128,512]{1,0:T(8,128)}, u32[]{:S(2)}) copy-start(f32[128,512]{1,0:T(8,128)} %convolution_subtract_fusion.17) | copy-start | bytes 786436
  83.1 8.8 %slice-start.1 = ((s8[6291456]{0:T(1024)(128)(4,1)}), s8[4194304]{0:T(1024)(128)(4,1)S(1)}, s32[]{:S(2)}) async-start(s8[6291456]{0:T(1024)(128)(4,1)} %bitcast.613), calls=%async_computation.3 | async-start | bytes 8388608
  87.4 8.2 %copy-start.8 = (bf16[2,2,24,512]{3,2,1,0:T(8,128)(2,1)S(1)}, bf16[2,2,24,512]{3,2,1,0:T(8,128)(2,1)}, u32[]{:S(2)}) copy-start(bf16[2,2,24,512]{3,2,1,0:T(8,128)(2,1)} %param.12) | copy-start | bytes 294916
  131.0 7.9 %collective-permute-start.3 = (bf16[2,128,512]{2,1,0:T(8,128)(2,1)S(1)}, bf16[2,128,512]{2,1,0:T(8,128)(2,1)S(1)}, u32[]{:S(2)}, u32[]{:S(2)}) collective-permute-start(bf16[2,128,512]{2,1,0:T(8,128)(2,1)S(1)} %get-tuple-element.10), channel_id=1, source_target_pairs={{4,0},{8,4},{12,8},{16,12},{20,16},{24,20},{28,24},{0,28},{5,1},{9... | collective-permute-start | bytes 786440 | tf_op jit(solution)/shard_map/ppermute | solution.py:19
  136.0 9.1 %collective-permute-start.2 = (bf16[2,128,512]{2,1,0:T(8,128)(2,1)S(1)}, bf16[2,128,512]{2,1,0:T(8,128)(2,1)S(1)}, u32[]{:S(2)}, u32[]{:S(2)}) collective-permute-start(bf16[2,128,512]{2,1,0:T(8,128)(2,1)S(1)} %get-tuple-element.9), channel_id=1, source_target_pairs={{0,4},{4,8},{8,12},{12,16},{16,20},{20,24},{24,28},{28,0},{1,5},{5... | collective-permute-start | bytes 786440 | tf_op jit(solution)/shard_map/ppermute | solution.py:18
  145.9 2.4 copy-start.3
  146.2 77.1 %copy-start.10 = (f32[64]{0:T(128)S(1)}, f32[64]{0:T(128)}, u32[]{:S(2)}) copy-start(f32[64]{0:T(128)} %param.18) | copy-start | bytes 772
  147.0 85.0 %slice-start.2 = ((s8[6291456]{0:T(1024)(128)(4,1)}), s8[2097152]{0:T(1024)(128)(4,1)S(1)}, s32[]{:S(2)}) async-start(s8[6291456]{0:T(1024)(128)(4,1)} %bitcast.615), calls=%async_computation.4 | async-start | bytes 4194304
  223.2 8.7 %slice-start.3 = ((s8[6291456]{0:T(1024)(128)(4,1)}), s8[4194304]{0:T(1024)(128)(4,1)S(1)}, s32[]{:S(2)}) async-start(s8[6291456]{0:T(1024)(128)(4,1)} %bitcast.615), calls=%async_computation.5 | async-start | bytes 8388608
  229.2 38.0 %copy-start.9 = (bf16[2,2,24,512]{3,2,1,0:T(8,128)(2,1)S(1)}, bf16[2,2,24,512]{3,2,1,0:T(8,128)(2,1)}, u32[]{:S(2)}) copy-start(bf16[2,2,24,512]{3,2,1,0:T(8,128)(2,1)} %param.12) | copy-start | bytes 294916
  271.5 5.0 %copy-start.11 = (s32[64]{0:T(128)S(1)}, s32[64]{0:T(128)}, u32[]{:S(2)}) copy-start(s32[64]{0:T(128)} %param.19) | copy-start | bytes 772
  272.0 7.7 %collective-permute-start.5 = (bf16[2,128,512]{2,1,0:T(8,128)(2,1)S(1)}, bf16[2,128,512]{2,1,0:T(8,128)(2,1)S(1)}, u32[]{:S(2)}, u32[]{:S(2)}) collective-permute-start(bf16[2,128,512]{2,1,0:T(8,128)(2,1)S(1)} %fusion.67), channel_id=1, source_target_pairs={{4,0},{8,4},{12,8},{16,12},{20,16},{24,20},{28,24},{0,28},{5,1},{9... | collective-permute-start | bytes 786440 | tf_op jit(solution)/shard_map/ppermute | solution.py:19
  275.4 9.1 %collective-permute-start.4 = (bf16[2,128,512]{2,1,0:T(8,128)(2,1)S(1)}, bf16[2,128,512]{2,1,0:T(8,128)(2,1)S(1)}, u32[]{:S(2)}, u32[]{:S(2)}) collective-permute-start(bf16[2,128,512]{2,1,0:T(8,128)(2,1)S(1)} %fusion.69), channel_id=1, source_target_pairs={{0,4},{4,8},{8,12},{12,16},{16,20},{20,24},{24,28},{28,0},{1,5},{5... | collective-permute-start | bytes 786440 | tf_op jit(solution)/shard_map/ppermute | solution.py:18
Sparse Core Ops, SparseCore 0:
  150.0 66.4 all-reduce.1
where the time goes:
time: 294 us; the launch traced here: 293 us
  blocking collectives  98.5 us (34%)
  waiting for transfers between devices  80.4 us (27%)
  matrix products  64.3 us (22%)
  starting transfers between devices  19.5 us (7%)
  between operations  15.3 us (5%)
  other arithmetic  8.67 us (3%)
  local copies, waits for them, and re-layouts  6.31 us (2%)
    psum x1, waiting for transfers between devices, per_device(): summed_focal = lax.psum(jnp.stack([focal_re, focal_im]), 'tile')  66.4 us
    dot_general x140, matrix products, plain_dot(): lax.dot_general(left, right, (((1,), (contract,)), ((), ())), preferred_e...  64.1 us
    all_gather x2, blocking collectives, per_device(): fold_shard_piece = lax.all_gather(coeff, 'tile', axis=2, tiled=True)  62 us
    all_gather x1, blocking collectives, apply_transpose(): shard_piece = lax.all_gather(projected, 'tile', axis=2, tiled=True)  30.7 us
    ppermute x3, starting transfers between devices, extended(): after = lax.ppermute(initial, axis, down)  13.3 us
    ppermute x3, waiting for transfers between devices, extended(): before = lax.ppermute(last, axis, up)  10.7 us
    all_to_all x1, starting transfers between devices, per_device(): lax.all_to_all(masked, 'tile', split_axis=1, concat_axis=2, tiled=True)  6 us
  transfers between devices with their start and end apart: 8, of which 5 were waited for; matrix products, arithmetic and copies ran while one was open for 13% of the time, Pallas kernels for 0%

commit v1 on v0

--- a/solution.py
+++ b/solution.py
@@ -6,6 +6,12 @@
 TILE = 512
 RANK = 24
 DAMPING = 0.8
+
+
+def add_all(block, name):
+    parts = lax.all_gather(block, name, axis=0, tiled=False)
+    total = parts.sum(axis=0)
+    return total
 
 
 def extended(x, sides, width):
@@ -186,7 +192,7 @@
     first_slot = lax.axis_index("tile") * slots_here
     sources = src_rows * lax.axis_size("src")
     permute = (focal_owner[:, None] == jnp.arange(focal_count)[None, :]).astype(jnp.float32)
-    summed_focal = lax.psum(jnp.stack([focal_re, focal_im]), "tile")
+    summed_focal = add_all(jnp.stack([focal_re, focal_im]), "tile")
     intensity = lax.psum(
         jnp.sum(summed_focal[0] * summed_focal[0] + summed_focal[1] * summed_focal[1], axis=0),
         "src",

time: 294 us -> 238 us (0.81)
  waiting for transfers between devices: 80.4 us -> 13.3 us
  blocking collectives: 98.5 us -> 130 us
  between operations: 15.3 us -> 1.93 us
  matrix products: 64.3 us -> 61.1 us
    psum x1 -> x0, waiting for transfers between devices: 66.4 us -> none  [per_device(): summed_focal = lax.psum(jnp.stack([focal_re, focal_im]), 'tile')]
    all_gather x0 -> x1, blocking collectives: none -> 31.4 us  [add_all(): parts = lax.all_gather(block, name, axis=0, tiled=False)]
    dot_general x140, matrix products: 64.1 us -> 60.9 us  [plain_dot(): lax.dot_general(left, right, (((1,), (contract,)), ((), ())), preferred_e...]
  transfers between devices with their start and end apart: 8 -> 7, of which waited for: 5 -> 4; matrix products, arithmetic and copies ran while one was open for 13% -> 16% of each run, Pallas kernels for 0% -> 0%
where the time goes in v1:
time: 238 us; the launch traced here: 237 us
  blocking collectives  130 us (55%)
  matrix products  61.1 us (26%)
  starting transfers between devices  18.3 us (8%)
  waiting for transfers between devices  13.3 us (6%)
  other arithmetic  7.3 us (3%)
  local copies, waits for them, and re-layouts  5.4 us (2%)
    all_gather x2, blocking collectives, per_device(): fold_shard_piece = lax.all_gather(coeff, 'tile', axis=2, tiled=True)  62 us
    dot_general x140, matrix products, plain_dot(): lax.dot_general(left, right, (((1,), (contract,)), ((), ())), preferred_e...  60.9 us
    all_gather x1, blocking collectives, add_all(): parts = lax.all_gather(block, name, axis=0, tiled=False)  31.4 us
    all_gather x1, blocking collectives, apply_transpose(): shard_piece = lax.all_gather(projected, 'tile', axis=2, tiled=True)  30.6 us
    ppermute x3, starting transfers between devices, extended(): after = lax.ppermute(initial, axis, down)  11 us
    ppermute x3, waiting for transfers between devices, extended(): before = lax.ppermute(last, axis, up)  9.73 us
    all_to_all x1, starting transfers between devices, per_device(): lax.all_to_all(masked, 'tile', split_axis=1, concat_axis=2, tiled=True)  6 us
    psum x1, blocking collectives, per_device(): lax.psum(jnp.sum(summed_focal[0] * summed_focal[0] + summed_focal[1] * su...  5.85 us
  transfers between devices with their start and end apart: 7, of which 4 were waited for; matrix products, arithmetic and copies ran while one was open for 16% of the time, Pallas kernels for 0%

profile of v1, /device:TPU:0, one launch (start us, length us, event | category | flops | bytes accessed | tf_op | source)
XLA Modules:
  0.0 237.2 jit_solution(13388173700304325301)
XLA Ops:
  0.7 1.9 fusion.459
  2.6 6.0 %collective-permute-start.1 = (bf16[2,128,512]{2,1,0:T(8,128)(2,1)}, bf16[2,128,512]{2,1,0:T(8,128)(2,1)}, u32[]{:S(2)}, u32[]{:S(2)}) collective-permute-start(bf16[2,128,512]{2,1,0:T(8,128)(2,1)} %get-tuple-element.12), channel_id=1, source_target_pairs={{4,0},{8,4},{12,8},{16,12},{20,16},{24,20},{28,24},{0,28},{5,1},{9... | collective-permute-start | bytes 786440 | tf_op jit(solution)/shard_map/ppermute | solution.py:25
  13.2 6.0 %all-to-all-start = ((bf16[8,2,2304]{2,1,0:T(2,128)(2,1)}), bf16[8,2,2304]{2,1,0:T(2,128)(2,1)}, u32[]{:S(2)}, u32[]{:S(2)}) async-start(bf16[8,2,2304]{2,1,0:T(2,128)(2,1)} %reshape.85), calls=%async_computation | async-start | bytes 147456 | tf_op jit(solution)/shard_map/all_to_all | solution.py:72
  28.2 31.3 %all_gather.15 = bf16[2,128,384]{1,2,0:T(8,128)(2,1)S(1)} all-gather(bf16[2,128,48]{1,2,0:T(8,128)(2,1)S(1)} %pad_maximum_fusion.6), channel_id=1, replica_groups=mesh['tile'=8,'src'=4] {'tile'}, dimensions={2}, use_global_device_ids=true | all-gather | bytes 221184 | tf_op jit(solution)/shard_map/all_gather | solution.py:150
  59.8 1.3 fusion.94
  61.1 1.3 fusion.112
  77.1 1.5 fusion.85
  78.6 1.6 fusion.175
  80.2 1.5 fusion.20
  81.7 1.5 fusion.22
  84.6 1.3 fusion.167
  89.9 30.7 %all_gather.16 = bf16[2,128,384]{1,2,0:T(8,128)(2,1)S(1)} all-gather(bf16[2,128,48]{1,2,0:T(8,128)(2,1)S(1)} %pad_maximum_fusion.7), channel_id=1, replica_groups=mesh['tile'=8,'src'=4] {'tile'}, dimensions={2}, use_global_device_ids=true | all-gather | bytes 221184 | tf_op jit(solution)/shard_map/all_gather | solution.py:150
  124.0 4.0 %collective-permute-start.3 = (bf16[2,128,512]{2,1,0:T(8,128)(2,1)S(1)}, bf16[2,128,512]{2,1,0:T(8,128)(2,1)S(1)}, u32[]{:S(2)}, u32[]{:S(2)}) collective-permute-start(bf16[2,128,512]{2,1,0:T(8,128)(2,1)S(1)} %get-tuple-element.10), channel_id=1, source_target_pairs={{4,0},{8,4},{12,8},{16,12},{20,16},{24,20},{28,24},{0,28},{5,1},{9... | collective-permute-start | bytes 786440 | tf_op jit(solution)/shard_map/ppermute | solution.py:25
  130.9 1.4 collective-permute-done.3
  132.5 6.0 %collective-permute-done.2 = bf16[2,128,512]{2,1,0:T(8,128)(2,1)S(1)} collective-permute-done((bf16[2,128,512]{2,1,0:T(8,128)(2,1)S(1)}, bf16[2,128,512]{2,1,0:T(8,128)(2,1)S(1)}, u32[]{:S(2)}, u32[]{:S(2)}) %collective-permute-start.2) | collective-permute-done | bytes 262176 | tf_op jit(solution)/shard_map/ppermute | solution.py:24
  142.6 31.4 %all-gather = f32[16,128,64]{1,2,0:T(8,128)S(1)} all-gather(f32[2,128,64]{1,2,0:T(8,128)S(1)} %pad_maximum_fusion.5), channel_id=2, replica_groups=mesh['tile'=8,'src'=4] {'tile'}, dimensions={0}, use_global_device_ids=true | all-gather | bytes 589824 | tf_op jit(solution)/shard_map/all_gather | solution.py:12
  174.2 5.8 %psum.7 = f32[64]{0:T(128)S(1)} all-reduce(f32[64]{0:T(128)S(1)} %add_reduce_fusion), channel_id=1, replica_groups=mesh['tile'=8,'src'=4] {'src'}, use_global_device_ids=true, to_apply=%region_2.3 | all-reduce | flops 64 | bytes 512 | tf_op jit(solution)/shard_map/psum | solution.py:196
  181.4 1.3 fusion.106
  182.8 1.3 fusion.160
  184.1 1.3 fusion.116
  189.6 30.6 %all_gather.19 = bf16[2,128,384]{1,2,0:T(8,128)(2,1)S(1)} all-gather(bf16[2,128,48]{1,2,0:T(8,128)(2,1)S(1)} %pad_maximum_fusion.8), channel_id=1, replica_groups=mesh['tile'=8,'src'=4] {'tile'}, dimensions={2}, use_global_device_ids=true | all-gather | bytes 221184 | tf_op jit(solution)/shard_map/all_gather | solution.py:114
  229.7 2.2 collective-permute-done.5
  231.8 3.7 %collective-permute-done.4 = bf16[2,128,512]{2,1,0:T(8,128)(2,1)S(1)} collective-permute-done((bf16[2,128,512]{2,1,0:T(8,128)(2,1)S(1)}, bf16[2,128,512]{2,1,0:T(8,128)(2,1)S(1)}, u32[]{:S(2)}, u32[]{:S(2)}) %collective-permute-start.4) | collective-permute-done | bytes 262176 | tf_op jit(solution)/shard_map/ppermute | solution.py:24
  235.7 1.6 fusion.61
  (216 shorter events, 58.4 us)
Async XLA Ops:
  0.6 62.4 %copy-start.1 = (bf16[2,128,1024]{2,1,0:T(8,128)(2,1)S(1)}, bf16[2,128,1024]{2,1,0:T(8,128)(2,1)}, u32[]{:S(2)}) copy-start(bf16[2,128,1024]{2,1,0:T(8,128)(2,1)} %param.10) | copy-start | bytes 1572868
  0.6 62.0 %copy-start.2 = (bf16[2,2,24,512]{3,2,1,0:T(8,128)(2,1)S(1)}, bf16[2,2,24,512]{3,2,1,0:T(8,128)(2,1)}, u32[]{:S(2)}) copy-start(bf16[2,2,24,512]{3,2,1,0:T(8,128)(2,1)} %param.13) | copy-start | bytes 294916
  2.6 74.5 %collective-permute-start.1 = (bf16[2,128,512]{2,1,0:T(8,128)(2,1)}, bf16[2,128,512]{2,1,0:T(8,128)(2,1)}, u32[]{:S(2)}, u32[]{:S(2)}) collective-permute-start(bf16[2,128,512]{2,1,0:T(8,128)(2,1)} %get-tuple-element.12), channel_id=1, source_target_pairs={{4,0},{8,4},{12,8},{16,12},{20,16},{24,20},{28,24},{0,28},{5,1},{9... | collective-permute-start | bytes 786440 | tf_op jit(solution)/shard_map/ppermute | solution.py:25
  8.6 70.0 %collective-permute-start = (bf16[2,128,512]{2,1,0:T(8,128)(2,1)}, bf16[2,128,512]{2,1,0:T(8,128)(2,1)}, u32[]{:S(2)}, u32[]{:S(2)}) collective-permute-start(bf16[2,128,512]{2,1,0:T(8,128)(2,1)} %get-tuple-element.11), channel_id=1, source_target_pairs={{0,4},{4,8},{8,12},{12,16},{16,20},{20,24},{24,28},{28,0},{1,5},{5... | collective-permute-start | bytes 786440 | tf_op jit(solution)/shard_map/ppermute | solution.py:24
  13.2 62.4 %all-to-all-start = ((bf16[8,2,2304]{2,1,0:T(2,128)(2,1)}), bf16[8,2,2304]{2,1,0:T(2,128)(2,1)}, u32[]{:S(2)}, u32[]{:S(2)}) async-start(bf16[8,2,2304]{2,1,0:T(2,128)(2,1)} %reshape.85), calls=%async_computation | async-start | bytes 147456 | tf_op jit(solution)/shard_map/all_to_all | solution.py:72
  19.2 46.6 %copy-start = (bf16[2,3,2,512,512]{4,3,2,1,0:T(8,128)(2,1)S(1)}, bf16[2,3,2,512,512]{4,3,2,1,0:T(8,128)(2,1)}, u32[]{:S(2)}) copy-start(bf16[2,3,2,512,512]{4,3,2,1,0:T(8,128)(2,1)} %param.11) | copy-start | bytes 18874372
  71.6 14.4 %slice-start = ((s8[6291456]{0:T(1024)(128)(4,1)}), s8[2097152]{0:T(1024)(128)(4,1)S(1)}, s32[]{:S(2)}) async-start(s8[6291456]{0:T(1024)(128)(4,1)} %bitcast.614), calls=%async_computation.1 | async-start | bytes 4194304
  77.0 8.9 %slice-start.1 = ((s8[6291456]{0:T(1024)(128)(4,1)}), s8[4194304]{0:T(1024)(128)(4,1)S(1)}, s32[]{:S(2)}) async-start(s8[6291456]{0:T(1024)(128)(4,1)} %bitcast.614), calls=%async_computation.2 | async-start | bytes 8388608
  77.1 8.9 %copy-start.6 = (f32[128,512]{1,0:T(8,128)S(1)}, f32[128,512]{1,0:T(8,128)}, u32[]{:S(2)}) copy-start(f32[128,512]{1,0:T(8,128)} %convolution_subtract_fusion.23) | copy-start | bytes 786436
  77.1 8.9 %copy-start.7 = (f32[128,512]{1,0:T(8,128)S(1)}, f32[128,512]{1,0:T(8,128)}, u32[]{:S(2)}) copy-start(f32[128,512]{1,0:T(8,128)} %fusion.3) | copy-start | bytes 786436
  77.1 10.1 %copy-start.4 = (f32[128,512]{1,0:T(8,128)S(1)}, f32[128,512]{1,0:T(8,128)}, u32[]{:S(2)}) copy-start(f32[128,512]{1,0:T(8,128)} %convolution_subtract_fusion.16) | copy-start | bytes 786436
  77.1 10.1 %copy-start.5 = (f32[128,512]{1,0:T(8,128)S(1)}, f32[128,512]{1,0:T(8,128)}, u32[]{:S(2)}) copy-start(f32[128,512]{1,0:T(8,128)} %convolution_subtract_fusion.17) | copy-start | bytes 786436
  80.2 8.4 %copy-start.8 = (bf16[2,2,24,512]{3,2,1,0:T(8,128)(2,1)S(1)}, bf16[2,2,24,512]{3,2,1,0:T(8,128)(2,1)}, u32[]{:S(2)}) copy-start(bf16[2,2,24,512]{3,2,1,0:T(8,128)(2,1)} %param.12) | copy-start | bytes 294916
  124.0 8.3 %collective-permute-start.3 = (bf16[2,128,512]{2,1,0:T(8,128)(2,1)S(1)}, bf16[2,128,512]{2,1,0:T(8,128)(2,1)S(1)}, u32[]{:S(2)}, u32[]{:S(2)}) collective-permute-start(bf16[2,128,512]{2,1,0:T(8,128)(2,1)S(1)} %get-tuple-element.10), channel_id=1, source_target_pairs={{4,0},{8,4},{12,8},{16,12},{20,16},{24,20},{28,24},{0,28},{5,1},{9... | collective-permute-start | bytes 786440 | tf_op jit(solution)/shard_map/ppermute | solution.py:25
  129.0 9.6 %collective-permute-start.2 = (bf16[2,128,512]{2,1,0:T(8,128)(2,1)S(1)}, bf16[2,128,512]{2,1,0:T(8,128)(2,1)S(1)}, u32[]{:S(2)}, u32[]{:S(2)}) collective-permute-start(bf16[2,128,512]{2,1,0:T(8,128)(2,1)S(1)} %get-tuple-element.9), channel_id=1, source_target_pairs={{0,4},{4,8},{8,12},{12,16},{16,20},{20,24},{24,28},{28,0},{1,5},{5... | collective-permute-start | bytes 786440 | tf_op jit(solution)/shard_map/ppermute | solution.py:24
  139.3 2.4 %copy-start.3 = (bf16[2,64,1024]{2,1,0:T(8,128)(2,1)S(1)}, bf16[2,64,1024]{2,1,0:T(8,128)(2,1)}, u32[]{:S(2)}) copy-start(bf16[2,64,1024]{2,1,0:T(8,128)(2,1)} %param.17) | copy-start | bytes 786436
  139.8 40.2 %copy-start.9 = (f32[64]{0:T(128)S(1)}, f32[64]{0:T(128)}, u32[]{:S(2)}) copy-start(f32[64]{0:T(128)} %param.18) | copy-start | bytes 772
  140.4 45.1 %slice-start.2 = ((s8[6291456]{0:T(1024)(128)(4,1)}), s8[2097152]{0:T(1024)(128)(4,1)S(1)}, s32[]{:S(2)}) async-start(s8[6291456]{0:T(1024)(128)(4,1)} %bitcast.616), calls=%async_computation.3 | async-start | bytes 4194304
  180.0 5.5 %slice-start.3 = ((s8[6291456]{0:T(1024)(128)(4,1)}), s8[4194304]{0:T(1024)(128)(4,1)S(1)}, s32[]{:S(2)}) async-start(s8[6291456]{0:T(1024)(128)(4,1)} %bitcast.616), calls=%async_computation.4 | async-start | bytes 8388608
  225.0 3.8 %copy-start.10 = (s32[64]{0:T(128)S(1)}, s32[64]{0:T(128)}, u32[]{:S(2)}) copy-start(s32[64]{0:T(128)} %param.19) | copy-start | bytes 772
  225.4 6.4 %collective-permute-start.5 = (bf16[2,128,512]{2,1,0:T(8,128)(2,1)S(1)}, bf16[2,128,512]{2,1,0:T(8,128)(2,1)S(1)}, u32[]{:S(2)}, u32[]{:S(2)}) collective-permute-start(bf16[2,128,512]{2,1,0:T(8,128)(2,1)S(1)} %fusion.67), channel_id=1, source_target_pairs={{4,0},{8,4},{12,8},{16,12},{20,16},{24,20},{28,24},{0,28},{5,1},{9... | collective-permute-start | bytes 786440 | tf_op jit(solution)/shard_map/ppermute | solution.py:25
  226.4 9.1 %collective-permute-start.4 = (bf16[2,128,512]{2,1,0:T(8,128)(2,1)S(1)}, bf16[2,128,512]{2,1,0:T(8,128)(2,1)S(1)}, u32[]{:S(2)}, u32[]{:S(2)}) collective-permute-start(bf16[2,128,512]{2,1,0:T(8,128)(2,1)S(1)} %fusion.69), channel_id=1, source_target_pairs={{0,4},{4,8},{8,12},{12,16},{16,20},{20,24},{24,28},{28,0},{1,5},{5... | collective-permute-start | bytes 786440 | tf_op jit(solution)/shard_map/ppermute | solution.py:24
